TPU v7x, 256 devices: a whole 4x4x8 slice. The times are simulated.
256 devices in a mesh: seq: 32 (over z_hi, y, core), fsdp: 8 (over z_lo, x).
Axes of the slice: x: 4, y: 4, z: 8 (z_hi: 4, z_lo: 2; z = z_hi * 2 + z_lo), core: 2. Of those that a mesh axis runs over, the one named last changes fastest.
Arguments:
- tokens: bfloat16 [32768, 1280], P('seq'), may hold values from -64 to 64
- cotangent: bfloat16 [32768, 1280], P('seq'), may hold values from -6 to 6
- raster_dest: int32 [32768], P('seq'), may hold values from 0 to 32767, as said below
- keep_mask: int32 [512, 16, 4096], P('seq', 'fsdp'), may hold values 0 or 1
- qkv_weight: bfloat16 [1280, 3840], P('seq', 'fsdp'), may hold values from -0.15625 to 0.15625
- out_weight: bfloat16 [1280, 1280], P('seq', 'fsdp'), may hold values from -0.15625 to 0.15625
Outputs:
- attended: bfloat16 [32768, 1280], P('seq', 'fsdp')
- grad_tokens: bfloat16 [32768, 1280], P('seq', 'fsdp')
- grad_qkv: float32 [1280, 3840], P('seq', 'fsdp')
- grad_out: float32 [1280, 1280], P('seq', 'fsdp')
Inputs may be any that keep to these rules, and one draw needn't show every extreme that they name: `raster_dest`: A permutation. Raster rows form bands of 2048 rows (8 patch rows of 256 patches); band b holds 32 windows of 8 by 8 patches, which go one to each block of 1024 window-order rows, in an order drawn for each band; inside its block, band b's window takes rows b * 64 to (b + 1) * 64 - 1, its patches in raster order.
All inputs are finite; a program needn't handle non-finite values. No bound on the sum of `keep_mask` on one device may be relied on, other than what follows from the above.
Results may differ from a plain program's by a relative error of at most 0.025.
The roundings to bfloat16 on the way count: a program that leaves them out, or rounds other values in their place, can miss the bound.
Values may be sent and summed in bfloat16 or wider, within the bound.
No kernel may reach another device: no remote copies, remote signals or barrier semaphores. Data moves between devices by JAX's collectives and lax.ppermute only.
A program may use at most 64 MiB of HBM per device.

v0:
```python
import jax
import jax.numpy as jnp
from jax import lax
from jax.sharding import PartitionSpec as P

HEAD_DIM = 80
WIN = 8
WIN_TOK = 64
INV_KEEP = 1.0 / 0.9


def to_half(values):
    return lax.optimization_barrier(values.astype(jnp.bfloat16))


def head_total(partial_value):
    rounded = to_half(partial_value).astype(jnp.float32)
    return lax.psum_scatter(
        rounded.astype(jnp.bfloat16), "fsdp", scatter_dimension=1, tiled=True
    ).astype(jnp.float32)


def per_device(tokens, cotangent, raster_dest, keep_mask, qkv_weight, out_weight):
    seq_count = lax.axis_size("seq")
    tok_dev = tokens.shape[0]
    score_scale = HEAD_DIM ** (-0.5)
    windows_local = tok_dev // WIN_TOK
    heads_local = keep_mask.shape[1]
    send_order = jnp.argsort(raster_dest)
    back_order = jnp.argsort(send_order)
    slot_index = jnp.arange(tok_dev, dtype=jnp.int32)
    band_index = slot_index // WIN_TOK
    patch_row = slot_index % WIN_TOK // WIN
    source = (band_index * WIN_TOK * seq_count + patch_row * WIN * seq_count) // tok_dev
    recv_slot = jnp.argsort(source * tok_dev + slot_index)
    slot_recv = jnp.argsort(recv_slot)

    def restore(window_rows):
        outgoing = window_rows[recv_slot]
        returned = lax.all_to_all(outgoing, "seq", split_axis=0, concat_axis=0, tiled=True)
        return returned[back_order]

    qkv_full, out_full = (
        lax.all_gather(qkv_weight, "seq", axis=0, tiled=True),
        lax.all_gather(out_weight, "seq", axis=0, tiled=True),
    )
    windowed = lax.all_to_all(tokens[send_order], "seq", split_axis=0, concat_axis=0, tiled=True)[
        slot_recv
    ]
    cot_window = lax.all_to_all(
        cotangent[send_order], "seq", split_axis=0, concat_axis=0, tiled=True
    )[slot_recv]
    projected = jnp.dot(windowed, qkv_full, preferred_element_type=jnp.float32).astype(jnp.bfloat16)
    unpacked = projected.reshape(windows_local, WIN_TOK, heads_local, 3, HEAD_DIM)
    queries = unpacked[:, :, :, 0].transpose(0, 2, 1, 3)
    key_rows = unpacked[:, :, :, 1].transpose(0, 2, 1, 3)
    value_rows = unpacked[:, :, :, 2].transpose(0, 2, 1, 3)
    keep_scale = (
        keep_mask.reshape(windows_local, heads_local, WIN_TOK, WIN_TOK).astype(jnp.float32)
        * INV_KEEP
    )
    scores = (
        jnp.einsum("whqe,whke->whqk", queries, key_rows, preferred_element_type=jnp.float32)
        * score_scale
    )
    attn_probs = jax.nn.softmax(scores, axis=-1)
    dropped = (attn_probs * keep_scale).astype(jnp.bfloat16)
    mixed = jnp.einsum(
        "whqk,whke->whqe", dropped, value_rows, preferred_element_type=jnp.float32
    ).astype(jnp.bfloat16)
    mixed_heads = mixed.transpose(0, 2, 1, 3).reshape(tok_dev, heads_local * HEAD_DIM)
    contract = (((1,), (1,)), ((), ()))
    out_partial = lax.dot_general(
        mixed_heads, out_full, contract, preferred_element_type=jnp.float32
    )
    attended = restore(head_total(out_partial).astype(jnp.bfloat16))
    grad_heads = jnp.dot(cot_window, out_full, preferred_element_type=jnp.float32).astype(
        jnp.bfloat16
    )
    grad_rows = grad_heads.reshape(windows_local, WIN_TOK, heads_local, HEAD_DIM).transpose(
        0, 2, 1, 3
    )
    grad_probs = (
        jnp.einsum("whqe,whke->whqk", grad_rows, value_rows, preferred_element_type=jnp.float32)
        * keep_scale
    )
    inner = jnp.sum(grad_probs * attn_probs, axis=-1, keepdims=True)
    grad_scores = (score_scale * attn_probs * (grad_probs - inner)).astype(jnp.bfloat16)
    grad_query = jnp.einsum(
        "whqk,whke->whqe", grad_scores, key_rows, preferred_element_type=jnp.float32
    )
    grad_key = jnp.einsum(
        "whqk,whqe->whke", grad_scores, queries, preferred_element_type=jnp.float32
    )
    grad_value = jnp.einsum(
        "whqk,whqe->whke", dropped, grad_rows, preferred_element_type=jnp.float32
    )
    stacked = jnp.stack([grad_query, grad_key, grad_value], axis=3)
    grad_projected = (
        stacked.transpose(0, 2, 1, 3, 4)
        .reshape(tok_dev, 3 * heads_local * HEAD_DIM)
        .astype(jnp.bfloat16)
    )
    back_partial = lax.dot_general(
        grad_projected, qkv_full, contract, preferred_element_type=jnp.float32
    )
    grad_tokens = restore(head_total(back_partial).astype(jnp.bfloat16))
    over_rows = (((0,), (0,)), ((), ()))
    grad_qkv_local = lax.dot_general(
        windowed, grad_projected, over_rows, preferred_element_type=jnp.float32
    )
    grad_out_local = lax.dot_general(
        cot_window, mixed_heads, over_rows, preferred_element_type=jnp.float32
    )
    grad_qkv, grad_out = (
        lax.psum_scatter(grad_qkv_local, "seq", scatter_dimension=0, tiled=True),
        lax.psum_scatter(grad_out_local, "seq", scatter_dimension=0, tiled=True),
    )
    grad_scale = (tok_dev * seq_count) ** (-0.5)
    return (attended, grad_tokens, grad_qkv * grad_scale, grad_out * grad_scale)


def solution(mesh):
    return jax.shard_map(
        per_device,
        mesh=mesh,
        in_specs=(
            P("seq", None),
            P("seq", None),
            P("seq"),
            P("seq", "fsdp", None),
            P("seq", "fsdp"),
            P("seq", "fsdp"),
        ),
        out_specs=(P("seq", "fsdp"), P("seq", "fsdp"), P("seq", "fsdp"), P("seq", "fsdp")),
        check_vma=False,
    )
```

profile of v0, /device:TPU:2, one launch (start us, length us, event | category | flops | bytes accessed | tf_op | source)
XLA Modules:
  0.0 583.5 jit_solution(13186685068350491355)
XLA Ops:
  7.2 5.2 sort.59
  12.4 5.5 gather_fusion.4
  17.9 11.6 %all-to-all-start.2 = ((bf16[32,32,1280]{2,1,0:T(8,128)(2,1)}), bf16[32,32,1280]{2,1,0:T(8,128)(2,1)}, u32[]{:S(2)}, u32[]{:S(2)}) async-start(bf16[32,32,1280]{2,1,0:T(8,128)(2,1)} %bitcast.90), calls=%async_computation.2 | async-start | bytes 5242880 | tf_op jit(solution)/shard_map/all_to_all | solution.py:50
  29.5 8.7 %gather_fusion = bf16[1024,1280]{1,0:T(8,128)(2,1)} fusion(bf16[1024,1280]{1,0:T(8,128)(2,1)} %param.6, s32[1024]{0:T(1024)S(1)} %fusion.29), kind=kCustom, calls=%fused_computation | custom fusion | bytes 5246976 | tf_op jit(solution)/shard_map/gather | solution.py:47
  38.2 50.0 %all-to-all-done.2 = bf16[32,32,1280]{2,1,0:T(8,128)(2,1)} async-done(((bf16[32,32,1280]{2,1,0:T(8,128)(2,1)}), bf16[32,32,1280]{2,1,0:T(8,128)(2,1)}, u32[]{:S(2)}, u32[]{:S(2)}) %all-to-all-start.2) | async-done | bytes 2621472 | tf_op jit(solution)/shard_map/all_to_all | solution.py:50
  88.2 8.7 %all-to-all-start = ((bf16[32,32,1280]{2,1,0:T(8,128)(2,1)}), bf16[32,32,1280]{2,1,0:T(8,128)(2,1)}, u32[]{:S(2)}, u32[]{:S(2)}) async-start(bf16[32,32,1280]{2,1,0:T(8,128)(2,1)} %bitcast.89), calls=%async_computation | async-start | bytes 5242880 | tf_op jit(solution)/shard_map/all_to_all | solution.py:47
  99.1 1.6 reshape.113
  100.7 2.6 copy.35
  103.3 4.4 sort.60
  107.6 4.4 sort.61
  112.0 87.9 %all_gather.7 = bf16[1280,160]{1,0:T(8,128)(2,1)S(1)} all-gather(bf16[40,160]{1,0:T(8,128)(2,1)S(1)} %copy-done.8), channel_id=1, replica_groups=mesh['seq'=32,'fsdp'=8] {'seq'}, dimensions={0}, use_global_device_ids=true | all-gather | bytes 422400 | tf_op jit(solution)/shard_map/all_gather | solution.py:45
  199.9 8.8 %gather_fusion.5 = bf16[1024,1280]{1,0:T(8,128)(2,1)} fusion(bf16[1024,1280]{1,0:T(8,128)(2,1)} %bitcast.12, s32[1024]{0:T(1024)S(1)} %fusion.30), kind=kCustom, calls=%fused_computation.5 | custom fusion | bytes 5246976 | tf_op jit(solution)/shard_map/gather | solution.py:50
  208.7 3.5 convolution_convert_fusion.7
  212.2 2.3 reshape.36
  214.6 2.4 copy.39
  217.0 8.7 %gather_fusion.1 = bf16[1024,1280]{1,0:T(8,128)(2,1)} fusion(bf16[1024,1280]{1,0:T(8,128)(2,1)} %bitcast.1, s32[1024]{0:T(1024)S(1)} %fusion.30), kind=kCustom, calls=%fused_computation.1 | custom fusion | bytes 5246976 | tf_op jit(solution)/shard_map/gather | solution.py:47
  225.7 4.5 convolution_convert_fusion.2
  230.2 3.8 reshape.34
  234.0 2.9 fusion.45
  236.9 2.4 copy.56
  239.3 2.4 copy.55
  241.8 2.4 copy.54
  244.2 2.7 fusion.46
  246.9 2.4 multiply_reduce_fusion
  253.0 4.2 copy.43
  257.2 3.9 convert_element_type.53
  261.1 4.8 convolution_convert_fusion
  265.9 4.5 copy.50
  270.5 2.3 fusion.3
  272.8 2.4 copy.38
  275.3 2.3 reshape.35
  277.5 3.4 convolution_convert_fusion.1
  280.9 4.5 copy.48
  286.4 3.7 fusion.52
  290.2 5.1 fusion.51
  295.4 19.4 %reduce-scatter.15.cloned.1.call-done = bf16[160,1024]{1,0:T(8,128)(2,1)} async-done(((bf16[1280,1024]{1,0:T(8,128)(2,1)}), bf16[160,1024]{1,0:T(8,128)(2,1)}) %reduce-scatter.15.cloned.1.call-update) | async-done | bytes 327696
  315.9 4.9 gather_fusion.6
  320.8 9.0 %all-to-all-start.3 = ((bf16[32,32,160]{2,1,0:T(8,128)(2,1)}), bf16[32,32,160]{2,1,0:T(8,128)(2,1)S(1)}, u32[]{:S(2)}, u32[]{:S(2)}) async-start(bf16[32,32,160]{2,1,0:T(8,128)(2,1)} %bitcast.95), calls=%async_computation.3 | async-start | bytes 1048576 | tf_op jit(solution)/shard_map/all_to_all | solution.py:40
  329.8 4.4 sort.62
  334.2 38.6 %reduce-scatter.13.cloned.1.call-done = bf16[160,1024]{1,0:T(8,128)(2,1)} async-done(((bf16[1280,1024]{1,0:T(8,128)(2,1)}), bf16[160,1024]{1,0:T(8,128)(2,1)}) %reduce-scatter.13.cloned.1.call-update) | async-done | bytes 327696
  372.8 2.0 copy.49
  374.7 5.7 gather_fusion.2
  380.4 9.1 %all-to-all-start.1 = ((bf16[32,32,160]{2,1,0:T(8,128)(2,1)}), bf16[32,32,160]{2,1,0:T(8,128)(2,1)}, u32[]{:S(2)}, u32[]{:S(2)}) async-start(bf16[32,32,160]{2,1,0:T(8,128)(2,1)} %bitcast.94), calls=%async_computation.1 | async-start | bytes 1048576 | tf_op jit(solution)/shard_map/all_to_all | solution.py:40
  389.6 78.1 %reduce-scatter.11.cloned.1.call-done = f32[40,160]{1,0:T(8,128)} async-done(((f32[1280,160]{1,0:T(8,128)}), f32[40,160]{1,0:T(8,128)}) %reduce-scatter.11.cloned.1.call-update) | async-done | bytes 25616 | tf_op jit(solution)/shard_map/reduce_scatter | solution.py:117
  469.1 94.0 %reduce-scatter.9.cloned.1.call-done = f32[40,480]{1,0:T(8,128)} async-done(((f32[1280,480]{1,0:T(8,128)}), f32[40,480]{1,0:T(8,128)}) %reduce-scatter.9.cloned.1.call-update) | async-done | bytes 76816 | tf_op jit(solution)/shard_map/reduce_scatter | solution.py:116
  564.6 4.9 gather_fusion.7
  569.5 1.9 copy.45
  571.4 4.6 gather_fusion.3
  (51 shorter events, 11.9 us)
Async XLA Ops:
  7.2 5.2 copy-start
  17.9 70.3 %all-to-all-start.2 = ((bf16[32,32,1280]{2,1,0:T(8,128)(2,1)}), bf16[32,32,1280]{2,1,0:T(8,128)(2,1)}, u32[]{:S(2)}, u32[]{:S(2)}) async-start(bf16[32,32,1280]{2,1,0:T(8,128)(2,1)} %bitcast.90), calls=%async_computation.2 | async-start | bytes 5242880 | tf_op jit(solution)/shard_map/all_to_all | solution.py:50
  88.2 128.7 %all-to-all-start = ((bf16[32,32,1280]{2,1,0:T(8,128)(2,1)}), bf16[32,32,1280]{2,1,0:T(8,128)(2,1)}, u32[]{:S(2)}, u32[]{:S(2)}) async-start(bf16[32,32,1280]{2,1,0:T(8,128)(2,1)} %bitcast.89), calls=%async_computation | async-start | bytes 5242880 | tf_op jit(solution)/shard_map/all_to_all | solution.py:47
  96.9 15.1 %copy-start.8 = (bf16[40,160]{1,0:T(8,128)(2,1)S(1)}, bf16[40,160]{1,0:T(8,128)(2,1)}, u32[]{:S(2)}) copy-start(bf16[40,160]{1,0:T(8,128)(2,1)} %param.11) | copy-start | bytes 38404
  96.9 128.7 %all-gather.2.cloned.1.call-start = ((), (), s32[]{:S(2)}) async-start(), calls=%async_computation.8 | async-start | bytes 1351680 | tf_op jit(solution)/shard_map/all_gather | solution.py:44
  97.7 217.1 %reduce-scatter.15.cloned.1.call-start = ((), (), s32[]{:S(2)}) async-start(), calls=%async_computation.12 | async-start | bytes 2949120
  246.9 2.5 copy-start.2
  246.9 2.5 copy-start.7
  249.3 1.1 copy-start.5
  249.4 1.3 copy-start.4
  249.8 1.2 copy-start.1
  249.8 1.3 copy-start.3
  270.5 102.3 %reduce-scatter.13.cloned.1.call-start = ((), (), s32[]{:S(2)}) async-start(), calls=%async_computation.11 | async-start | bytes 2949120
  285.4 1.0 copy-start.6
  285.5 182.2 %reduce-scatter.11.cloned.1.call-start = ((), (), s32[]{:S(2)}) async-start(), calls=%async_computation.10 | async-start | bytes 1351680 | tf_op jit(solution)/shard_map/reduce_scatter | solution.py:117
  290.2 272.9 %reduce-scatter.9.cloned.1.call-start = ((), (), s32[]{:S(2)}) async-start(), calls=%async_computation.9 | async-start | bytes 2703360 | tf_op jit(solution)/shard_map/reduce_scatter | solution.py:116
  320.8 59.6 %all-to-all-start.3 = ((bf16[32,32,160]{2,1,0:T(8,128)(2,1)}), bf16[32,32,160]{2,1,0:T(8,128)(2,1)S(1)}, u32[]{:S(2)}, u32[]{:S(2)}) async-start(bf16[32,32,160]{2,1,0:T(8,128)(2,1)} %bitcast.95), calls=%async_computation.3 | async-start | bytes 1048576 | tf_op jit(solution)/shard_map/all_to_all | solution.py:40
  380.4 191.0 %all-to-all-start.1 = ((bf16[32,32,160]{2,1,0:T(8,128)(2,1)}), bf16[32,32,160]{2,1,0:T(8,128)(2,1)}, u32[]{:S(2)}, u32[]{:S(2)}) async-start(bf16[32,32,160]{2,1,0:T(8,128)(2,1)} %bitcast.94), calls=%async_computation.1 | async-start | bytes 1048576 | tf_op jit(solution)/shard_map/all_to_all | solution.py:40
Sparse Core Ops, SparseCore 0:
  100.3 68.3 all-gather.1
  270.6 44.1 reduce-scatter.14
  317.3 55.4 reduce-scatter.12
  376.4 91.1 reduce-scatter.10
  471.9 91.1 reduce-scatter.8
where the time goes:
time: 585 us; the launch traced here: 583 us
  waiting for transfers between devices  281 us (48%)
  local copies, waits for them, and re-layouts  104 us (18%)
  blocking collectives  87.9 us (15%)
  starting transfers between devices  38.6 us (7%)
  matrix products  33.5 us (6%)
  other arithmetic  24.6 us (4%)
  between operations  14 us (2%)
    reduce_scatter x1, waiting for transfers between devices, per_device(): lax.psum_scatter(grad_qkv_local, 'seq', scatter_dimension=0, tiled=True)  94 us
    all_gather x1, blocking collectives, per_device(): lax.all_gather(out_weight, 'seq', axis=0, tiled=True)  87.9 us
    reduce_scatter x1, waiting for transfers between devices, per_device(): lax.psum_scatter(grad_out_local, 'seq', scatter_dimension=0, tiled=True)  78.1 us
    unnamed x7, waiting for transfers between devices  58.7 us
    all_to_all x1, waiting for transfers between devices, per_device(): lax.all_to_all(cotangent[send_order], 'seq', split_axis=0, concat_axis=0,...  50 us
    unnamed x27, local copies, waits for them, and re-layouts  23.8 us
    all_to_all x2, starting transfers between devices, restore(): lax.all_to_all(outgoing, 'seq', split_axis=0, concat_axis=0, tiled=True)  18.1 us
  transfers between devices with their start and end apart: 9, of which 5 were waited for; matrix products, arithmetic and copies ran while one was open for 17% of the time, Pallas kernels for 0%

commit v1 on v0

--- a/solution.py
+++ b/solution.py
@@ -7,6 +7,19 @@
 WIN = 8
 WIN_TOK = 64
 INV_KEEP = 1.0 / 0.9
+
+
+def part_shards(row_data, shard_axis):
+    main = jnp.concatenate(
+        lax.all_to_all(
+            jnp.stack([row_data] * lax.axis_size(shard_axis)),
+            axis_name=shard_axis,
+            split_axis=0,
+            concat_axis=0,
+        ),
+        axis=0,
+    )
+    return main
 
 
 def to_half(values):
@@ -42,7 +55,7 @@
 
     qkv_full, out_full = (
         lax.all_gather(qkv_weight, "seq", axis=0, tiled=True),
-        lax.all_gather(out_weight, "seq", axis=0, tiled=True),
+        part_shards(out_weight, "seq"),
     )
     windowed = lax.all_to_all(tokens[send_order], "seq", split_axis=0, concat_axis=0, tiled=True)[
         slot_recv

time: 585 us -> 566 us (0.968)
  blocking collectives: 87.9 us -> 0 us
  waiting for transfers between devices: 281 us -> 341 us
    all_gather x1 -> x0, blocking collectives: 87.9 us -> none  [per_device(): lax.all_gather(out_weight, 'seq', axis=0, tiled=True)]
    all_to_all x1, waiting for transfers between devices: 0.01 us -> 26.8 us  [per_device(): lax.all_to_all(tokens[send_order], 'seq', split_axis=0, concat_axis=0, ti...]
    all_gather x1, waiting for transfers between devices: 0.01 us -> 23 us  [per_device(): lax.all_gather(qkv_weight, 'seq', axis=0, tiled=True)]
    all_to_all x0 -> x1, starting transfers between devices: none -> 11.5 us  [part_shards(): lax.all_to_all(jnp.stack([row_data] * lax.axis_size(shard_axis)), axis_na...]
    all_to_all x0 -> x1, waiting for transfers between devices: none -> 9.23 us  [part_shards(): lax.all_to_all(jnp.stack([row_data] * lax.axis_size(shard_axis)), axis_na...]
    unnamed x27 -> x25, local copies, waits for them, and re-layouts: 23.8 us -> 23.8 us
  transfers between devices with their start and end apart: 9 -> 10, of which waited for: 5 -> 8; matrix products, arithmetic and copies ran while one was open for 17% -> 20% of each run, Pallas kernels for 0% -> 0%
where the time goes in v1:
time: 566 us; the launch traced here: 564 us
  waiting for transfers between devices  341 us (60%)
  local copies, waits for them, and re-layouts  107 us (19%)
  starting transfers between devices  43 us (8%)
  matrix products  33.5 us (6%)
  other arithmetic  25.3 us (4%)
  between operations  14 us (2%)
    reduce_scatter x1, waiting for transfers between devices, per_device(): lax.psum_scatter(grad_qkv_local, 'seq', scatter_dimension=0, tiled=True)  93.8 us
    reduce_scatter x1, waiting for transfers between devices, per_device(): lax.psum_scatter(grad_out_local, 'seq', scatter_dimension=0, tiled=True)  77.9 us
    unnamed x7, waiting for transfers between devices  57.3 us
    all_to_all x1, waiting for transfers between devices, per_device(): lax.all_to_all(cotangent[send_order], 'seq', split_axis=0, concat_axis=0,...  53.5 us
    all_to_all x1, waiting for transfers between devices, per_device(): lax.all_to_all(tokens[send_order], 'seq', split_axis=0, concat_axis=0, ti...  26.8 us
    unnamed x25, local copies, waits for them, and re-layouts  23.8 us
    all_gather x1, waiting for transfers between devices, per_device(): lax.all_gather(qkv_weight, 'seq', axis=0, tiled=True)  23 us
    all_to_all x2, starting transfers between devices, restore(): lax.all_to_all(outgoing, 'seq', split_axis=0, concat_axis=0, tiled=True)  18.2 us
  transfers between devices with their start and end apart: 10, of which 8 were waited for; matrix products, arithmetic and copies ran while one was open for 20% of the time, Pallas kernels for 0%

profile of v1, /device:TPU:2, one launch (start us, length us, event | category | flops | bytes accessed | tf_op | source)
XLA Modules:
  0.0 564.2 jit_solution(10413388286708288582)
XLA Ops:
  8.9 11.5 %all-to-all-start.1 = ((bf16[32,40,160]{2,1,0:T(8,128)(2,1)}), bf16[32,40,160]{2,1,0:T(8,128)(2,1)S(1)}, u32[]{:S(2)}, u32[]{:S(2)}) async-start(bf16[32,40,160]{2,1,0:T(8,128)(2,1)} %stack.14), calls=%async_computation.1 | async-start | bytes 1310720 | tf_op jit(solution)/shard_map/all_to_all | solution.py:14
  20.5 5.1 sort.59
  25.5 5.5 gather_fusion.4
  31.0 9.2 %all-to-all-done.1 = bf16[32,40,160]{2,1,0:T(8,128)(2,1)S(1)} async-done(((bf16[32,40,160]{2,1,0:T(8,128)(2,1)}), bf16[32,40,160]{2,1,0:T(8,128)(2,1)S(1)}, u32[]{:S(2)}, u32[]{:S(2)}) %all-to-all-start.1) | async-done | bytes 409632 | tf_op jit(solution)/shard_map/all_to_all | solution.py:14
  40.2 6.1 %all-to-all-start.3 = ((bf16[32,32,1280]{2,1,0:T(8,128)(2,1)}), bf16[32,32,1280]{2,1,0:T(8,128)(2,1)}, u32[]{:S(2)}, u32[]{:S(2)}) async-start(bf16[32,32,1280]{2,1,0:T(8,128)(2,1)} %bitcast.91), calls=%async_computation.3 | async-start | bytes 5242880 | tf_op jit(solution)/shard_map/all_to_all | solution.py:63
  46.3 8.7 %gather_fusion = bf16[1024,1280]{1,0:T(8,128)(2,1)} fusion(bf16[1024,1280]{1,0:T(8,128)(2,1)} %param.6, s32[1024]{0:T(1024)S(1)} %fusion.29), kind=kCustom, calls=%fused_computation | custom fusion | bytes 5246976 | tf_op jit(solution)/shard_map/gather | solution.py:60
  55.0 53.5 %all-to-all-done.3 = bf16[32,32,1280]{2,1,0:T(8,128)(2,1)} async-done(((bf16[32,32,1280]{2,1,0:T(8,128)(2,1)}), bf16[32,32,1280]{2,1,0:T(8,128)(2,1)}, u32[]{:S(2)}, u32[]{:S(2)}) %all-to-all-start.3) | async-done | bytes 2621472 | tf_op jit(solution)/shard_map/all_to_all | solution.py:63
  108.5 7.1 %all-to-all-start = ((bf16[32,32,1280]{2,1,0:T(8,128)(2,1)}), bf16[32,32,1280]{2,1,0:T(8,128)(2,1)}, u32[]{:S(2)}, u32[]{:S(2)}) async-start(bf16[32,32,1280]{2,1,0:T(8,128)(2,1)} %bitcast.90), calls=%async_computation | async-start | bytes 5242880 | tf_op jit(solution)/shard_map/all_to_all | solution.py:60
  118.5 2.7 reshape.119
  121.2 2.6 copy.35
  123.7 4.4 sort.60
  128.1 4.4 sort.61
  132.5 8.9 %gather_fusion.5 = bf16[1024,1280]{1,0:T(8,128)(2,1)} fusion(bf16[1024,1280]{1,0:T(8,128)(2,1)} %bitcast.13, s32[1024]{0:T(1024)S(1)} %fusion.30), kind=kCustom, calls=%fused_computation.5 | custom fusion | bytes 5246976 | tf_op jit(solution)/shard_map/gather | solution.py:63
  141.4 3.5 convolution_convert_fusion.7
  144.9 2.3 reshape.42
  147.2 2.4 copy.39
  149.6 26.8 %all-to-all-done = bf16[32,32,1280]{2,1,0:T(8,128)(2,1)} async-done(((bf16[32,32,1280]{2,1,0:T(8,128)(2,1)}), bf16[32,32,1280]{2,1,0:T(8,128)(2,1)}, u32[]{:S(2)}, u32[]{:S(2)}) %all-to-all-start) | async-done | bytes 2621472 | tf_op jit(solution)/shard_map/all_to_all | solution.py:60
  176.3 8.7 %gather_fusion.1 = bf16[1024,1280]{1,0:T(8,128)(2,1)} fusion(bf16[1024,1280]{1,0:T(8,128)(2,1)} %bitcast.1, s32[1024]{0:T(1024)S(1)} %fusion.30), kind=kCustom, calls=%fused_computation.1 | custom fusion | bytes 5246976 | tf_op jit(solution)/shard_map/gather | solution.py:60
  185.0 23.0 %all-gather.2.cloned.1.call-done = bf16[1280,480]{1,0:T(8,128)(2,1)} async-done(((bf16[40,480]{1,0:T(8,128)(2,1)}), bf16[1280,480]{1,0:T(8,128)(2,1)}) %all-gather.2.cloned.1.call-update) | async-done | bytes 1228816 | tf_op jit(solution)/shard_map/all_gather | solution.py:57
  208.0 4.5 convolution_convert_fusion.2
  212.5 3.8 reshape.39
  216.4 2.9 fusion.45
  219.3 2.4 copy.56
  221.7 2.4 copy.55
  224.1 2.4 copy.54
  226.5 2.7 fusion.46
  229.2 2.4 multiply_reduce_fusion
  235.4 4.2 copy.43
  239.5 3.9 convert_element_type.53
  243.4 4.8 convolution_convert_fusion
  248.3 4.5 copy.50
  252.8 2.3 fusion.3
  255.2 2.4 copy.38
  259.9 3.4 convolution_convert_fusion.1
  263.3 4.5 copy.48
  268.7 3.7 fusion.52
  272.5 5.1 fusion.51
  277.6 17.7 %reduce-scatter.15.cloned.1.call-done = bf16[160,1024]{1,0:T(8,128)(2,1)} async-done(((bf16[1280,1024]{1,0:T(8,128)(2,1)}), bf16[160,1024]{1,0:T(8,128)(2,1)}) %reduce-scatter.15.cloned.1.call-update) | async-done | bytes 327696
  296.5 4.9 gather_fusion.6
  301.4 9.0 %all-to-all-start.4 = ((bf16[32,32,160]{2,1,0:T(8,128)(2,1)}), bf16[32,32,160]{2,1,0:T(8,128)(2,1)S(1)}, u32[]{:S(2)}, u32[]{:S(2)}) async-start(bf16[32,32,160]{2,1,0:T(8,128)(2,1)} %bitcast.98), calls=%async_computation.4 | async-start | bytes 1048576 | tf_op jit(solution)/shard_map/all_to_all | solution.py:53
  310.4 4.4 sort.62
  314.8 38.9 %reduce-scatter.13.cloned.1.call-done = bf16[160,1024]{1,0:T(8,128)(2,1)} async-done(((bf16[1280,1024]{1,0:T(8,128)(2,1)}), bf16[160,1024]{1,0:T(8,128)(2,1)}) %reduce-scatter.13.cloned.1.call-update) | async-done | bytes 327696
  355.7 5.7 %gather_fusion.2 = bf16[1024,160]{1,0:T(8,128)(2,1)} fusion(bf16[1024,160]{1,0:T(8,128)(2,1)} %copy.49, s32[1024]{0:T(1024)S(1)} %fusion.31), kind=kCustom, calls=%fused_computation.2 | custom fusion | bytes 659456 | tf_op jit(solution)/shard_map/gather | solution.py:52
  361.3 9.2 %all-to-all-start.2 = ((bf16[32,32,160]{2,1,0:T(8,128)(2,1)}), bf16[32,32,160]{2,1,0:T(8,128)(2,1)}, u32[]{:S(2)}, u32[]{:S(2)}) async-start(bf16[32,32,160]{2,1,0:T(8,128)(2,1)} %bitcast.97), calls=%async_computation.2 | async-start | bytes 1048576 | tf_op jit(solution)/shard_map/all_to_all | solution.py:53
  370.6 77.9 %reduce-scatter.11.cloned.1.call-done = f32[40,160]{1,0:T(8,128)} async-done(((f32[1280,160]{1,0:T(8,128)}), f32[40,160]{1,0:T(8,128)}) %reduce-scatter.11.cloned.1.call-update) | async-done | bytes 25616 | tf_op jit(solution)/shard_map/reduce_scatter | solution.py:130
  449.9 93.8 %reduce-scatter.9.cloned.1.call-done = f32[40,480]{1,0:T(8,128)} async-done(((f32[1280,480]{1,0:T(8,128)}), f32[40,480]{1,0:T(8,128)}) %reduce-scatter.9.cloned.1.call-update) | async-done | bytes 76816 | tf_op jit(solution)/shard_map/reduce_scatter | solution.py:129
  545.3 4.9 gather_fusion.7
  552.2 4.6 gather_fusion.3
  (51 shorter events, 20.7 us)
Async XLA Ops:
  7.2 18.3 %copy-start = (bf16[1024,1280]{1,0:T(8,128)(2,1)S(1)}, bf16[1024,1280]{1,0:T(8,128)(2,1)}, u32[]{:S(2)}) copy-start(bf16[1024,1280]{1,0:T(8,128)(2,1)} %param.7) | copy-start | bytes 7864324
  8.9 31.3 %all-to-all-start.1 = ((bf16[32,40,160]{2,1,0:T(8,128)(2,1)}), bf16[32,40,160]{2,1,0:T(8,128)(2,1)S(1)}, u32[]{:S(2)}, u32[]{:S(2)}) async-start(bf16[32,40,160]{2,1,0:T(8,128)(2,1)} %stack.14), calls=%async_computation.1 | async-start | bytes 1310720 | tf_op jit(solution)/shard_map/all_to_all | solution.py:14
  40.2 68.3 %all-to-all-start.3 = ((bf16[32,32,1280]{2,1,0:T(8,128)(2,1)}), bf16[32,32,1280]{2,1,0:T(8,128)(2,1)}, u32[]{:S(2)}, u32[]{:S(2)}) async-start(bf16[32,32,1280]{2,1,0:T(8,128)(2,1)} %bitcast.91), calls=%async_computation.3 | async-start | bytes 5242880 | tf_op jit(solution)/shard_map/all_to_all | solution.py:63
  108.5 67.9 %all-to-all-start = ((bf16[32,32,1280]{2,1,0:T(8,128)(2,1)}), bf16[32,32,1280]{2,1,0:T(8,128)(2,1)}, u32[]{:S(2)}, u32[]{:S(2)}) async-start(bf16[32,32,1280]{2,1,0:T(8,128)(2,1)} %bitcast.90), calls=%async_computation | async-start | bytes 5242880 | tf_op jit(solution)/shard_map/all_to_all | solution.py:60
  115.6 92.4 %all-gather.2.cloned.1.call-start = ((), (), s32[]{:S(2)}) async-start(), calls=%async_computation.9 | async-start | bytes 1351680 | tf_op jit(solution)/shard_map/all_gather | solution.py:57
  116.3 179.0 %reduce-scatter.15.cloned.1.call-start = ((), (), s32[]{:S(2)}) async-start(), calls=%async_computation.13 | async-start | bytes 2949120
  229.2 2.5 copy-start.2
  229.2 2.5 copy-start.7
  231.7 1.1 copy-start.5
  231.7 1.3 copy-start.4
  232.1 1.2 copy-start.1
  232.2 1.3 copy-start.3
  252.8 100.9 %reduce-scatter.13.cloned.1.call-start = ((), (), s32[]{:S(2)}) async-start(), calls=%async_computation.12 | async-start | bytes 2949120
  267.8 1.0 copy-start.6
  267.8 180.7 %reduce-scatter.11.cloned.1.call-start = ((), (), s32[]{:S(2)}) async-start(), calls=%async_computation.11 | async-start | bytes 1351680 | tf_op jit(solution)/shard_map/reduce_scatter | solution.py:130
  272.5 271.3 %reduce-scatter.9.cloned.1.call-start = ((), (), s32[]{:S(2)}) async-start(), calls=%async_computation.10 | async-start | bytes 2703360 | tf_op jit(solution)/shard_map/reduce_scatter | solution.py:129
  301.4 59.9 %all-to-all-start.4 = ((bf16[32,32,160]{2,1,0:T(8,128)(2,1)}), bf16[32,32,160]{2,1,0:T(8,128)(2,1)S(1)}, u32[]{:S(2)}, u32[]{:S(2)}) async-start(bf16[32,32,160]{2,1,0:T(8,128)(2,1)} %bitcast.98), calls=%async_computation.4 | async-start | bytes 1048576 | tf_op jit(solution)/shard_map/all_to_all | solution.py:53
  361.3 190.8 %all-to-all-start.2 = ((bf16[32,32,160]{2,1,0:T(8,128)(2,1)}), bf16[32,32,160]{2,1,0:T(8,128)(2,1)}, u32[]{:S(2)}, u32[]{:S(2)}) async-start(bf16[32,32,160]{2,1,0:T(8,128)(2,1)} %bitcast.97), calls=%async_computation.2 | async-start | bytes 1048576 | tf_op jit(solution)/shard_map/all_to_all | solution.py:53
Sparse Core Ops, SparseCore 0:
  118.9 89.0 all-gather.1
  252.9 42.3 reduce-scatter.14
  297.9 55.7 reduce-scatter.12
  357.3 91.1 reduce-scatter.10
  452.7 90.9 reduce-scatter.8
